TPU v7x, 32 devices: a whole 2x2x4 slice. The times are simulated.
32 devices in a mesh: lat: 4 (over y, x), lon: 8 (over z, core).
Axes of the slice: x: 2, y: 2, z: 4, core: 2. Of those that a mesh axis runs over, the one named last changes fastest.
Arguments:
- fields: bfloat16 [16, 720, 641], P('lat', 'lon'), may hold values from -36 to 36
- group_size: int32 [8], replicated, may hold values from 1 to 121, 641 in all
- band_of_row: int32 [16], P('lat'), may hold values from 0 to 7, never falling along the last dimension, each value on 1 to 4 neighbouring positions
- basis_spectra: float32 [8, 9, 8, 2, 361], replicated, may hold values from -0.75 to 0.75
- basis_coef: float32 [641, 8], replicated, may hold values from -5 to 5
- mlp_gain: float32 [641], replicated, may hold values from 0.25 to 1.75
- w_in: bfloat16 [641, 1282], replicated, may hold values from -0.25 to 0.25
- w_out: bfloat16 [1282, 641], replicated, may hold values from -0.15625 to 0.15625
Outputs:
- block_out: bfloat16 [16, 720, 641], P('lat', 'lon')
Inputs may be any that keep to these rules, and one draw needn't show every extreme that they name: `group_size`: group j holds the channels that follow those of groups 0 to j - 1; the sizes sum to 641. `band_of_row`: band numbers never fall along latitude; every band covers 1 to 4 rows.
All inputs are finite; a program needn't handle non-finite values.
Results may differ from a plain program's by a relative error of at most 0.0051.
Values may be sent and summed in bfloat16 or wider, within the bound.
A program may use at most 64 MiB of HBM per device.

v0:
```python
import functools
import math

import jax
import jax.numpy as jnp
import numpy as np
from jax import lax
from jax.experimental import pallas as pl
from jax.experimental.pallas import tpu as pltpu
from jax.sharding import PartitionSpec as P

HALO = 4
TAPS = 2 * HALO + 1
EPSILON = 1e-05
VMEM = pl.BlockSpec(memory_space=pltpu.VMEM)
SMEM = pl.BlockSpec(memory_space=pltpu.SMEM)
MESH = pl.DeviceIdType.MESH
DMA = pltpu.SemaphoreType.DMA
PARAMS = pltpu.CompilerParams(vmem_limit_bytes=60 * 1024 * 1024)


def round_up(value, step):
    return -(-value // step) * step


def dft_tables(lon_count, pieces, width, bins):
    cols = lon_count // pieces
    freq = lon_count // 2 + 1
    phase = np.arange(lon_count)[:, None] * np.arange(freq)[None, :] % lon_count
    angle = phase * (2.0 * math.pi / lon_count)
    cosine = np.cos(angle)
    sine = np.where(2 * phase % lon_count == 0, 0.0, np.sin(angle))
    index = np.arange(freq)
    weight = np.where((index == 0) | (2 * index == lon_count), 1.0, 2.0) / lon_count
    table = np.zeros((pieces, width, 2, bins), np.float64)
    table[:, :cols, 0, :freq] = cosine.reshape(pieces, cols, freq)
    table[:, :cols, 1, :freq] = -sine.reshape(pieces, cols, freq)
    table = table.reshape(pieces * width, 2 * bins).astype(jnp.bfloat16)
    total = table.astype(np.float64).sum(axis=0, keepdims=True).astype(np.float32)
    scaled = np.zeros((2, bins), np.float32)
    scaled[:, :freq] = weight
    return table, total, scaled.reshape(1, 2 * bins)


def place(index):
    pieces = lax.axis_size("lon")
    return (lax.div(index, pieces), lax.rem(index, pieces))


def greet(devices, me):
    barrier = pltpu.get_barrier_semaphore()

    def signal(step, carry):
        pl.semaphore_signal(
            barrier, inc=1, device_id=place(lax.rem(me + step, devices)), device_id_type=MESH
        )
        return carry

    lax.fori_loop(1, devices, signal, 0)
    pl.semaphore_wait(barrier, devices - 1)


def own_index():
    return lax.axis_index("lat") * lax.axis_size("lon") + lax.axis_index("lon")


def drain(blocks, amount, semaphore):
    part = blocks.at[pl.ds(0, amount)]
    pltpu.make_async_copy(part, part, semaphore).wait()


def group_rows(size_ref, lanes, groups):
    group = lax.rem(lax.broadcasted_iota(jnp.int32, (1, lanes), 1), groups)
    start = jnp.zeros((1, lanes), jnp.int32)
    size = jnp.zeros((1, lanes), jnp.int32)
    for index in range(groups):
        start = start + jnp.where(group > index, size_ref[index], 0)
        size = size + jnp.where(group == index, size_ref[index], 0)
    return start, size


def membership(first, chan, start, size):
    channel = first + lax.broadcasted_iota(jnp.int32, (chan, start.shape[1]), 0)
    return (channel >= start) & (channel < start + size)


def scatter_body(
    devices, active, freq, rows, cols, groups,
    size_ref, band_ref, block_ref, flat_ref, coef_ref, basis_ref,
    arrived_ref, reports_ref, kern_ref,
    report_ref,
    send_sem, recv_sem, report_send_sem, report_recv_sem, local_sem,
):
    me = own_index()
    greet(devices, me)

    def send(step, carry):
        target = lax.rem(me + step, devices)

        @pl.when(target < active)
        def _():
            pltpu.make_async_remote_copy(
                src_ref=block_ref.at[target],
                dst_ref=arrived_ref.at[me],
                send_sem=send_sem,
                recv_sem=recv_sem,
                device_id=place(target),
                device_id_type=MESH,
            ).start()

        return carry

    lax.fori_loop(1, devices, send, 0)
    own = pltpu.make_async_copy(
        block_ref.at[lax.rem(me, active)], arrived_ref.at[me], local_sem
    )
    own.start()

    chan = block_ref.shape[1]
    pixels = rows * cols
    lane = lax.broadcasted_iota(jnp.int32, (pixels, 128), 0)
    slot = lax.broadcasted_iota(jnp.int32, (pixels, 128), 1)
    segment = (lane >= slot * cols) & (lane < (slot + 1) * cols)
    segment = jnp.where(segment, 1.0, 0.0).astype(jnp.bfloat16)

    def add_up(cells):
        return jnp.dot(cells, segment, preferred_element_type=jnp.float32)

    cells = flat_ref[...]
    means = add_up(cells) / cols
    near = means.astype(jnp.bfloat16)
    spread_out = lax.dot_general(
        near, segment, (((1,), (1,)), ((), ())), preferred_element_type=jnp.float32
    )
    offset = cells.astype(jnp.float32) - spread_out
    square = offset * offset
    high = square.astype(jnp.bfloat16)
    low = (square - high.astype(jnp.float32)).astype(jnp.bfloat16)
    shift = means - near.astype(jnp.float32)
    squares = jnp.maximum(add_up(high) + add_up(low) - cols * shift * shift, 0.0)
    exact = functools.partial(
        lax.dot_general, precision=lax.Precision.HIGHEST, preferred_element_type=jnp.float32
    )
    over_chan = (((0,), (0,)), ((), ()))
    over_last = (((1,), (1,)), ((), ()))
    start, size = group_rows(size_ref, 128, groups)
    member = jnp.where(
        membership(0, active * chan, start, size)
        & (lax.broadcasted_iota(jnp.int32, (1, 128), 1) < groups),
        1.0, 0.0,
    )
    centre = exact(means, member, over_chan) / jnp.maximum(size, 1).astype(jnp.float32)
    offset = means - exact(member, centre, over_last)
    spread = exact(squares + cols * offset * offset, member, over_chan)
    rest = report_ref.shape[1] - 2 * rows * groups
    place_of = lax.broadcasted_iota(jnp.int32, (1, rest), 1)
    bands = jnp.zeros((1, rest), jnp.float32)
    for row in range(rows):
        bands = jnp.where(place_of == row, band_ref[row].astype(jnp.float32), bands)
    report = jnp.concatenate(
        [centre[row : row + 1, :groups] for row in range(rows)]
        + [spread[row : row + 1, :groups] for row in range(rows)]
        + [bands],
        axis=1,
    )
    report_ref[...] = report
    reports_ref[me] = report

    bins = kern_ref.shape[2]
    total = coef_ref.shape[1]
    wanted = me * chan + lax.broadcasted_iota(jnp.int32, (chan, total), 0)
    chosen = jnp.where(lax.broadcasted_iota(jnp.int32, (chan, total), 1) == wanted, 1.0, 0.0)
    coef = exact(chosen, coef_ref[...], over_last)
    high = coef.astype(jnp.bfloat16).astype(jnp.float32)
    coef = jnp.concatenate([high, coef - high, high], axis=1).astype(jnp.bfloat16)
    blank = jnp.zeros((basis_ref.shape[1], bins - freq), jnp.float32)

    def generate(n, carry):
        basis = jnp.concatenate(
            [basis_ref[n, :, 0, :], blank, basis_ref[n, :, 1, :], blank], axis=1
        )
        high = basis.astype(jnp.bfloat16).astype(jnp.float32)
        both = jnp.concatenate([high, high, basis - high], axis=0).astype(jnp.bfloat16)
        made = jnp.dot(coef, both, preferred_element_type=jnp.float32)
        kern_ref[n, :chan] = made[:, :bins]
        kern_ref[n, chan:] = made[:, bins:]
        return carry

    def tell(step, carry):
        pltpu.make_async_remote_copy(
            src_ref=report_ref,
            dst_ref=reports_ref.at[me],
            send_sem=report_send_sem,
            recv_sem=report_recv_sem,
            device_id=place(lax.rem(me + step, devices)),
            device_id_type=MESH,
        ).start()
        return carry

    early = basis_ref.shape[0] // 8
    lax.fori_loop(0, early, generate, 0, unroll=3)
    lax.fori_loop(1, devices, tell, 0)
    lax.fori_loop(early, basis_ref.shape[0], generate, 0, unroll=3)
    own.wait()
    drain(reports_ref, devices - 1, report_send_sem)
    drain(reports_ref, devices - 1, report_recv_sem)

    @pl.when(me < active)
    def _():
        drain(block_ref, active - 1, send_sem)
        drain(arrived_ref, devices - 1, recv_sem)

    @pl.when(me >= active)
    def _():
        drain(block_ref, active, send_sem)

        def clear(n, carry):
            arrived_ref[n] = jnp.zeros(arrived_ref.shape[1:], arrived_ref.dtype)
            return carry

        lax.fori_loop(0, devices, clear, 0)


def gather_body(devices, active, mixed_ref, returned_ref, send_sem, recv_sem, local_sem):
    me = own_index()
    greet(devices, me)

    @pl.when(me < active)
    def _():
        def send(step, carry):
            target = lax.rem(me + step, devices)
            pltpu.make_async_remote_copy(
                src_ref=mixed_ref.at[target],
                dst_ref=returned_ref.at[me],
                send_sem=send_sem,
                recv_sem=recv_sem,
                device_id=place(target),
                device_id_type=MESH,
            ).start()
            return carry

        lax.fori_loop(1, devices, send, 0)
        own = pltpu.make_async_copy(mixed_ref.at[me], returned_ref.at[me], local_sem)
        own.start()
        own.wait()
        drain(mixed_ref, devices - 1, send_sem)
        drain(returned_ref, active - 1, recv_sem)

    @pl.when(me >= active)
    def _():
        drain(returned_ref, active, recv_sem)


def corr_body(
    pieces, rows, cols, width, bins, groups,
    size_ref, block_ref, reports_ref, table_ref, total_ref, weight_ref, kern_ref,
    out_ref, wide_ref, spec_ref, prod_ref, corr_ref,
):
    chan = block_ref.shape[1]
    bands = block_ref.shape[0] // pieces
    lat = bands * rows
    lanes = reports_ref.shape[2]
    start, size = group_rows(size_ref, lanes, groups)
    amount = size.astype(jnp.float32) * cols
    lane = lax.broadcasted_iota(jnp.int32, (1, lanes), 1)
    member = membership(own_index() * chan, chan, start, size)
    means, scales, numbers = [], [], []
    for band in range(bands):
        report = reports_ref[band * pieces : (band + 1) * pieces, 0]
        centre = jnp.sum(report, axis=0, keepdims=True) / pieces
        offset = report - centre
        between = amount * jnp.sum(offset * offset, axis=0, keepdims=True)
        within = jnp.sum(report, axis=0, keepdims=True)
        for row in range(rows):
            low, high = row * groups, (rows + row) * groups
            here = member & (lane >= low) & (lane < low + groups)
            there = member & (lane >= high) & (lane < high + groups)

            def pick(mask, cells):
                return jnp.sum(jnp.where(mask, cells, 0.0), axis=1, keepdims=True)

            square = pick(here, between) + pick(there, within)
            count = pick(here, amount) * pieces
            means.append(pick(here, centre))
            scales.append(lax.rsqrt(square / jnp.maximum(count, 1.0) + EPSILON))
            mark = lane == 2 * rows * groups + row
            numbers.append(jnp.sum(jnp.where(mark, report[:1], 0.0)).astype(jnp.int32))
    wide_ref[...] = jnp.zeros_like(wide_ref)
    for band in range(bands):
        for piece in range(pieces):
            cells = block_ref[band * pieces + piece].astype(jnp.float32)
            for row in range(rows):
                at = (band * rows + row) * chan
                wide_ref[at : at + chan, piece * width : piece * width + cols] = cells[
                    :, row * cols : (row + 1) * cols
                ]
    raw = jnp.dot(
        wide_ref[...].astype(jnp.bfloat16), table_ref[...], preferred_element_type=jnp.float32
    )
    for row in range(lat):
        at = row * chan
        spec_ref[at : at + chan] = (raw[at : at + chan] - means[row] * total_ref[...]) * scales[row]
    for row in range(lat):
        band = numbers[row]
        real = jnp.zeros((chan, bins), jnp.float32)
        imag = jnp.zeros((chan, bins), jnp.float32)
        for tap in range(TAPS):
            source = row + tap - HALO
            if source < 0 or source >= lat:
                continue
            spec_real = spec_ref[source * chan : (source + 1) * chan, :bins]
            spec_imag = spec_ref[source * chan : (source + 1) * chan, bins:]
            kern_real = kern_ref[band * TAPS + tap, :chan]
            kern_imag = kern_ref[band * TAPS + tap, chan:]
            real = real + kern_real * spec_real - kern_imag * spec_imag
            imag = imag + kern_real * spec_imag + kern_imag * spec_real
        prod_ref[row * chan : (row + 1) * chan, :bins] = real
        prod_ref[row * chan : (row + 1) * chan, bins:] = imag
    corr_ref[...] = lax.dot_general(
        (prod_ref[...] * weight_ref[...]).astype(jnp.bfloat16),
        table_ref[...],
        (((1,), (1,)), ((), ())),
        preferred_element_type=jnp.float32,
    )
    for band in range(bands):
        for piece in range(pieces):
            parts = []
            for row in range(rows):
                at = (band * rows + row) * chan
                parts.append(
                    corr_ref[at : at + chan, piece * width : piece * width + cols]
                )
            cells = block_ref[band * pieces + piece].astype(jnp.float32)
            out_ref[band * pieces + piece] = (
                cells + jnp.concatenate(parts, axis=1)
            ).astype(jnp.bfloat16)


def per_device(fields, group_size, band_of_row, basis_spectra, basis_coef, mlp_gain, w_in, w_out):
    row_count, col_count, chan_count = fields.shape
    pieces = lax.axis_size("lon")
    bands = lax.axis_size("lat")
    devices = pieces * bands
    lon_count = col_count * pieces
    lat_count = row_count * bands
    freq_count = lon_count // 2 + 1
    groups = group_size.shape[0]
    pixels = row_count * col_count
    chan = round_up(-(-chan_count // devices), 8)
    active = -(-chan_count // chan)
    width = round_up(col_count, 128)
    bins = round_up(freq_count, 128)
    band_count, _, basis_count = basis_spectra.shape[:3]

    turned = jnp.transpose(fields, (2, 0, 1)).reshape(chan_count, pixels)
    turned = jnp.pad(turned, ((0, active * chan - chan_count), (0, 0)))

    lanes = round_up((2 * groups + 1) * row_count, 128)
    basis = basis_spectra.reshape(band_count * TAPS, basis_count, 2, freq_count)
    arrived, reports, kern = pl.pallas_call(
        functools.partial(
            scatter_body, devices, active, freq_count, row_count, col_count, groups
        ),
        out_shape=[
            jax.ShapeDtypeStruct((devices, chan, pixels), jnp.bfloat16),
            jax.ShapeDtypeStruct((devices, 1, lanes), jnp.float32),
            jax.ShapeDtypeStruct((band_count * TAPS, 2 * chan, bins), jnp.float32),
        ],
        in_specs=[SMEM] * 2 + [VMEM] * 4,
        out_specs=[VMEM] * 3,
        scratch_shapes=[
            pltpu.VMEM((1, lanes), jnp.float32),
        ]
        + [DMA] * 5,
        compiler_params=pltpu.CompilerParams(
            collective_id=0, has_side_effects=True, vmem_limit_bytes=60 * 1024 * 1024
        ),
    )(
        group_size,
        band_of_row,
        turned.reshape(active, chan, pixels),
        turned,
        basis_coef.T,
        basis,
    )
    table, sums, weight = dft_tables(lon_count, pieces, width, bins)
    mixed = pl.pallas_call(
        functools.partial(corr_body, pieces, row_count, col_count, width, bins, groups),
        out_shape=jax.ShapeDtypeStruct((devices, chan, pixels), jnp.bfloat16),
        in_specs=[SMEM] + [VMEM] * 6,
        out_specs=VMEM,
        scratch_shapes=[
            pltpu.VMEM((lat_count * chan, pieces * width), jnp.float32),
            pltpu.VMEM((lat_count * chan, 2 * bins), jnp.float32),
            pltpu.VMEM((lat_count * chan, 2 * bins), jnp.float32),
            pltpu.VMEM((lat_count * chan, pieces * width), jnp.float32),
        ],
        compiler_params=PARAMS,
    )(group_size, arrived, reports, table, sums, weight, kern)
    returned = pl.pallas_call(
        functools.partial(gather_body, devices, active),
        out_shape=jax.ShapeDtypeStruct((active, chan, pixels), jnp.bfloat16),
        in_specs=[VMEM],
        out_specs=VMEM,
        scratch_shapes=[DMA] * 3,
        compiler_params=pltpu.CompilerParams(
            collective_id=1, has_side_effects=True, vmem_limit_bytes=60 * 1024 * 1024
        ),
    )(mixed)
    inputs = returned.reshape(active * chan, pixels)[:chan_count].T.astype(jnp.float32)
    centre = jnp.mean(inputs, axis=-1, keepdims=True)
    spread = jnp.mean((inputs - centre) ** 2, axis=-1, keepdims=True)
    normalised = ((inputs - centre) * lax.rsqrt(spread + EPSILON) * mlp_gain).astype(jnp.bfloat16)
    hidden = jax.nn.gelu(
        jnp.dot(normalised, w_in, preferred_element_type=jnp.float32), approximate=False
    ).astype(jnp.bfloat16)
    result = inputs + jnp.dot(hidden, w_out, preferred_element_type=jnp.float32)
    return result.astype(jnp.bfloat16).reshape(row_count, col_count, chan_count)


def solution(mesh):
    placed = (P("lat", "lon", None), P(), P("lat"), P(), P(), P(), P(), P())
    return jax.shard_map(
        per_device, mesh=mesh, in_specs=placed, out_specs=P("lat", "lon", None), check_vma=False
    )
```

profile of v0, /device:TPU:0, one launch (start us, length us, event | category | flops | bytes accessed | tf_op | source)
XLA Modules:
  0.0 68.7 jit_solution(4799968776704455884)
XLA Ops:
  0.0 0.0 copy-start
  0.0 1.9 %copy.18 = bf16[641,4,90]{2,1,0:T(4,128)(2,1)S(1)} copy(bf16[641,4,90]{0,1,2:T(4,128)(2,1)} %bitcast.35) | data formatting | bytes 923040 | tf_op jit(solution)/shard_map/reshape | solution.py:355
  2.0 0.7 reshape.33
  2.6 0.8 %pad.4.flat_ref = bf16[648,360]{1,0:T(8,128)(2,1)} pad(bf16[641,360]{1,0:T(8,128)(2,1)S(1)} %reshape.33, bf16[]{:T(256)} %constant.36.clone.1), padding=0_7x0_0 | pad | bytes 928082 | tf_op jit(solution)/shard_map/jit(_pad)/pad | solution.py:356
  3.5 25.3 %shard_map.109 = (bf16[32,24,360]{2,1,0:T(8,128)(2,1)}, f32[32,1,128]{2,1,0:T(1,128)}, f32[72,48,384]{2,1,0:T(8,128)}) custom-call(s32[8]{0:T(128)} %size_ref.3, s32[4]{0:T(128)} %band_ref.1, bf16[27,24,360]{2,1,0:T(8,128)(2,1)} %bitcast.33, bf16[648,360]{1,0:T(8,128)(2,1)} %pad.4.flat_ref, f32[8,641]{1,0:T(8,128)} %bitcast.36, f32[72,8,2,361]{3,2,1,0:T(2,128)} %bitcast.34), custom_call_target="tpu_custom_call" | custom-call | tf_op jit(solution)/shard_map/pallas_call | solution.py:360
  28.8 7.7 %shard_map.110.mixed_ref = bf16[32,24,360]{2,1,0:T(8,128)(2,1)} custom-call(s32[8]{0:T(128)} %size_ref.3, bf16[32,24,360]{2,1,0:T(8,128)(2,1)} %get-tuple-element.8.block_ref, f32[32,1,128]{2,1,0:T(1,128)} %get-tuple-element.9.reports_ref, bf16[1024,768]{1,0:T(8,128)(2,1)} %constant.76.clone.table_ref, f32[1,768]{1,0:T(1,128)} %constant.77.clone.total_ref, ...), custom_call_target="tpu_custom_call" | custom-call | tf_op jit(solution)/shard_map/pallas_call | solution.py:387
  36.4 0.0 copy-start.1
  36.5 19.4 %shard_map.111 = bf16[27,24,360]{2,1,0:T(8,128)(2,1)} custom-call(bf16[32,24,360]{2,1,0:T(8,128)(2,1)} %shard_map.110.mixed_ref), custom_call_target="tpu_custom_call" | custom-call | tf_op jit(solution)/shard_map/pallas_call | solution.py:400
  55.9 1.2 %convert_reduce_fusion = f32[360]{0:T(512)S(1)} fusion(bf16[648,360]{1,0:T(8,128)(2,1)} %bitcast.30), kind=kLoop, calls=%fused_computation.21 | loop fusion | flops 461160 | bytes 462960 | tf_op jit(solution)/shard_map/reduce_sum | solution.py:411
  57.0 1.2 %fusion.14 = f32[360]{0:T(512)S(1)} fusion(f32[360]{0:T(512)S(1)} %broadcast_multiply_fusion, bf16[648,360]{1,0:T(8,128)(2,1)} %bitcast.31), kind=kLoop, calls=%fused_computation.26 | loop fusion | flops 922680 | bytes 464400 | tf_op jit(solution)/shard_map/reduce_sum | solution.py:412
  58.2 0.0 copy-done
  58.2 0.0 copy-done.1
  58.2 8.1 %fusion.10 = bf16[360,641]{0,1:T(8,128)(2,1)S(1)} fusion(bf16[1282,641]{0,1:T(8,128)(2,1)S(1)} %copy-done, bf16[641,1282]{1,0:T(8,128)(2,1)} %param.17, f32[641]{0:T(1024)S(1)} %copy-done.1, f32[360]{0:T(512)S(1)} %add_rsqrt_fusion, f32[360]{0:T(512)S(1)} %broadcast_multiply_fusion, bf16[648,360]{1,0:T(8,128)(2,1)} %bitcast.32), kind=kOutput, calls=%fused_computation.20 | convolution fusion | flops 1215181056 | bytes 4930584 | tf_op jit(solution)/shard_map/dot_general | solution.py:417
  66.3 0.8 %reshape.34 = bf16[4,90,641]{1,0,2:T(4,128)(2,1)S(1)} reshape(bf16[360,641]{0,1:T(8,128)(2,1)S(1)} %fusion.10) | data formatting | bytes 923040 | tf_op jit(solution)/shard_map/reshape | solution.py:418
  67.2 1.6 %copy.17 = bf16[4,90,641]{2,0,1:T(4,128)(2,1)} copy(bf16[4,90,641]{1,0,2:T(4,128)(2,1)S(1)} %reshape.34) | data formatting | bytes 923040 | tf_op jit(solution)/shard_map/reshape | solution.py:418
  (2 shorter events, 0.0 us)
Async XLA Ops:
  0.0 58.2 %copy-start = (bf16[1282,641]{0,1:T(8,128)(2,1)S(1)}, bf16[1282,641]{0,1:T(8,128)(2,1)}, u32[]{:S(2)}) copy-start(bf16[1282,641]{0,1:T(8,128)(2,1)} %param.18) | copy-start | bytes 4930576
  36.4 21.8 %copy-start.1 = (f32[641]{0:T(1024)S(1)}, f32[641]{0:T(1024)}, u32[]{:S(2)}) copy-start(f32[641]{0:T(1024)} %param.16) | copy-start | bytes 7696
where the time goes:
time: 69.1 us; the launch traced here: 68.7 us
  Pallas kernels  52.4 us (76%)
  matrix products  8.08 us (12%)
  local copies, waits for them, and re-layouts  5.84 us (8%)
  other arithmetic  2.38 us (3%)
    pallas_call x1, Pallas kernels, per_device(): pl.pallas_call(functools.partial(scatter_body, devices, active, freq_coun...  25.3 us
    pallas_call x1, Pallas kernels, per_device(): pl.pallas_call(functools.partial(gather_body, devices, active), out_shape...  19.4 us
    dot_general x1, matrix products, per_device(): result = inputs + jnp.dot(hidden, w_out, preferred_element_type=jnp.float32)  8.08 us
    pallas_call x1, Pallas kernels, per_device(): pl.pallas_call(functools.partial(corr_body, pieces, row_count, col_count,...  7.66 us
    reshape x2, local copies, waits for them, and re-layouts, per_device(): turned = jnp.transpose(fields, (2, 0, 1)).reshape(chan_count, pixels)  2.6 us
    reshape x2, local copies, waits for them, and re-layouts, per_device(): return result.astype(jnp.bfloat16).reshape(row_count, col_count, chan_count)  2.39 us

commit v1 on v0

v1 whole, which is shorter than its diff:
```python
import functools
import math

import jax
import jax.numpy as jnp
import numpy as np
from jax import lax
from jax.experimental import pallas as pl
from jax.experimental.pallas import tpu as pltpu
from jax.sharding import PartitionSpec as P

HALO = 4
TAPS = 2 * HALO + 1
EPSILON = 1e-05
SUB = 8
VMEM = pl.BlockSpec(memory_space=pltpu.VMEM)
SMEM = pl.BlockSpec(memory_space=pltpu.SMEM)
ANY = pl.BlockSpec(memory_space=pl.ANY)
MESH = pl.DeviceIdType.MESH
DMA = pltpu.SemaphoreType.DMA


def round_up(value, step):
    return -(-value // step) * step


def dft_tables(lon_count, bins):
    freq = lon_count // 2 + 1
    phase = np.arange(lon_count)[:, None] * np.arange(freq)[None, :] % lon_count
    angle = phase * (2.0 * math.pi / lon_count)
    cosine = np.cos(angle)
    sine = np.where(2 * phase % lon_count == 0, 0.0, np.sin(angle))
    index = np.arange(freq)
    weight = np.where((index == 0) | (2 * index == lon_count), 1.0, 2.0) / lon_count
    table = np.zeros((lon_count, 2, bins), np.float64)
    table[:, 0, :freq] = cosine
    table[:, 1, :freq] = -sine
    table = table.reshape(lon_count, 2 * bins).astype(jnp.bfloat16)
    total = table.astype(np.float64).sum(axis=0, keepdims=True).astype(np.float32)
    scaled = np.zeros((2, bins), np.float32)
    scaled[:, :freq] = weight
    return table, total, scaled.reshape(1, 2 * bins)


def pixel_order(rows, cols):
    pixels = rows * cols
    index = np.arange(pixels)
    order = np.zeros((pixels, pixels), np.float32)
    order[index, index % rows * cols + index // rows] = 1.0
    return order.astype(jnp.bfloat16)


def place(index):
    pieces = lax.axis_size("lon")
    return (lax.div(index, pieces), lax.rem(index, pieces))


def own_index():
    return lax.axis_index("lat") * lax.axis_size("lon") + lax.axis_index("lon")


def drain(blocks, amount, semaphore):
    part = blocks.at[pl.ds(0, amount)]
    pltpu.make_async_copy(part, part, semaphore).wait()


def group_rows(size_ref, lanes, groups):
    group = lax.rem(lax.broadcasted_iota(jnp.int32, (1, lanes), 1), groups)
    start = jnp.zeros((1, lanes), jnp.int32)
    size = jnp.zeros((1, lanes), jnp.int32)
    for index in range(groups):
        start = start + jnp.where(group > index, size_ref[index], 0)
        size = size + jnp.where(group == index, size_ref[index], 0)
    return start, size


def membership(first, chan, start, size):
    channel = first + lax.broadcasted_iota(jnp.int32, (chan, start.shape[1]), 0)
    return (channel >= start) & (channel < start + size)


exact = functools.partial(
    lax.dot_general, precision=lax.Precision.HIGHEST, preferred_element_type=jnp.float32
)
OVER_FIRST = (((0,), (0,)), ((), ()))
OVER_LAST = (((1,), (1,)), ((), ()))


def block_body(
    devices, homes, chan, freq, bins, rows, cols, chan_count, groups,
    size_ref, band_ref,
    x_hbm, order_hbm, coef_hbm, basis_hbm, table_hbm, total_hbm, weight_hbm, gain_hbm,
    win_hbm, wout_hbm,
    out_ref,
    x_ref, order_ref, coef_ref, basis_ref, table_ref, total_ref, weight_ref, gain_ref,
    win_ref, wout_ref,
    flat_ref, arrived_ref, mixed_ref, returned_ref, report_ref, reports_ref,
    kern_ref, wide_ref, spec_ref, prod_ref, corr_ref,
    load_sem, block_send_sem, block_recv_sem, report_send_sem, report_recv_sem,
    mixed_send_sem, mixed_recv_sem, local_sem,
):
    me = own_index()
    pieces = lax.axis_size("lon")
    bands = devices // pieces
    lat = bands * rows
    parts = chan // SUB
    pixels = rows * cols
    band_count = basis_ref.shape[0] // TAPS
    own_home = lax.div(me * homes + devices - 1, devices)
    own_home = lax.rem(own_home, homes)
    is_home = lax.div(own_home * devices, homes) == me

    def device_of(home):
        return lax.div(home * devices, homes)

    loads = [
        pltpu.make_async_copy(source, target, load_sem.at[index])
        for index, (source, target) in enumerate(
            [
                (x_hbm, x_ref), (order_hbm, order_ref), (coef_hbm, coef_ref),
                (basis_hbm, basis_ref), (table_hbm, table_ref), (total_hbm, total_ref),
                (weight_hbm, weight_ref), (gain_hbm, gain_ref), (win_hbm, win_ref),
                (wout_hbm, wout_ref),
            ]
        )
    ]
    for load in loads:
        load.start()
    barrier = pltpu.get_barrier_semaphore()

    def greet(step, carry):
        pl.semaphore_signal(
            barrier, inc=1, device_id=place(lax.rem(me + step, devices)), device_id_type=MESH
        )
        return carry

    lax.fori_loop(1, devices, greet, 0)
    loads[0].wait()
    loads[1].wait()
    x = x_ref[...].reshape(pixels, chan_count)
    turned = lax.dot_general(
        x, order_ref[...], OVER_FIRST, preferred_element_type=jnp.float32
    ).astype(jnp.bfloat16)
    flat_ref[...] = jnp.zeros_like(flat_ref)
    flat_ref[:chan_count] = turned
    pl.semaphore_wait(barrier, devices - 1)

    def send_part(part):
        def send(step, carry):
            home = lax.rem(own_home + step, homes)
            target = device_of(home)

            @pl.when(target != me)
            def _():
                pltpu.make_async_remote_copy(
                    src_ref=flat_ref.at[pl.ds(pl.multiple_of(home * chan + part * SUB, SUB), SUB)],
                    dst_ref=arrived_ref.at[part, me],
                    send_sem=block_send_sem,
                    recv_sem=block_recv_sem.at[part],
                    device_id=place(target),
                    device_id_type=MESH,
                ).start()

            return carry

        lax.fori_loop(0, homes, send, 0)

    send_part(0)

    @pl.when(is_home)
    def _():
        for part in range(parts):
            first = pl.multiple_of(own_home * chan + part * SUB, SUB)
            pltpu.make_async_copy(
                flat_ref.at[pl.ds(first, SUB)], arrived_ref.at[part, me], local_sem.at[part]
            ).start()

    lane = lax.broadcasted_iota(jnp.int32, (pixels, 128), 0)
    slot = lax.broadcasted_iota(jnp.int32, (pixels, 128), 1)
    segment = (lane >= slot * cols) & (lane < (slot + 1) * cols)
    segment = jnp.where(segment, 1.0, 0.0).astype(jnp.bfloat16)

    def add_up(cells):
        return jnp.dot(cells, segment, preferred_element_type=jnp.float32)

    cells = flat_ref[...]
    means = add_up(cells) / cols
    near = means.astype(jnp.bfloat16)
    spread_out = lax.dot_general(near, segment, OVER_LAST, preferred_element_type=jnp.float32)
    offset = cells.astype(jnp.float32) - spread_out
    square = offset * offset
    high = square.astype(jnp.bfloat16)
    low = (square - high.astype(jnp.float32)).astype(jnp.bfloat16)
    shift = means - near.astype(jnp.float32)
    squares = jnp.maximum(add_up(high) + add_up(low) - cols * shift * shift, 0.0)
    start, size = group_rows(size_ref, 128, groups)
    member = jnp.where(
        membership(0, homes * chan, start, size)
        & (lax.broadcasted_iota(jnp.int32, (1, 128), 1) < groups),
        1.0, 0.0,
    )
    centre = exact(means, member, OVER_FIRST) / jnp.maximum(size, 1).astype(jnp.float32)
    offset = means - exact(member, centre, OVER_LAST)
    spread = exact(squares + cols * offset * offset, member, OVER_FIRST)
    lanes = report_ref.shape[1]
    rest = lanes - 2 * rows * groups
    place_of = lax.broadcasted_iota(jnp.int32, (1, rest), 1)
    numbers = jnp.zeros((1, rest), jnp.float32)
    for row in range(rows):
        numbers = jnp.where(place_of == row, band_ref[row].astype(jnp.float32), numbers)
    report = jnp.concatenate(
        [centre[row : row + 1, :groups] for row in range(rows)]
        + [spread[row : row + 1, :groups] for row in range(rows)]
        + [numbers],
        axis=1,
    )
    report_ref[...] = report
    reports_ref[me] = report

    for part in range(1, parts):
        send_part(part)

    def tell(step, carry):
        pltpu.make_async_remote_copy(
            src_ref=report_ref,
            dst_ref=reports_ref.at[me],
            send_sem=report_send_sem,
            recv_sem=report_recv_sem,
            device_id=place(lax.rem(me + step, devices)),
            device_id_type=MESH,
        ).start()
        return carry

    lax.fori_loop(1, devices, tell, 0)

    loads[2].wait()
    loads[3].wait()
    wanted = own_home * chan + lax.broadcasted_iota(jnp.int32, (chan, chan_count), 0)
    chosen = jnp.where(
        lax.broadcasted_iota(jnp.int32, (chan, chan_count), 1) == wanted, 1.0, 0.0
    )
    coef = exact(chosen, coef_ref[...], OVER_LAST)
    high = coef.astype(jnp.bfloat16).astype(jnp.float32)
    coef = jnp.concatenate([high, coef - high, high], axis=1).astype(jnp.bfloat16)
    blank = jnp.zeros((basis_ref.shape[1], bins - freq), jnp.float32)

    def generate(n, carry):
        basis = jnp.concatenate(
            [basis_ref[n, :, 0, :], blank, basis_ref[n, :, 1, :], blank], axis=1
        )
        high = basis.astype(jnp.bfloat16).astype(jnp.float32)
        both = jnp.concatenate([high, high, basis - high], axis=0).astype(jnp.bfloat16)
        made = jnp.dot(coef, both, preferred_element_type=jnp.float32)
        kern_ref[n, :chan] = made[:, :bins]
        kern_ref[n, chan:] = made[:, bins:]
        return carry

    lax.fori_loop(0, basis_ref.shape[0], generate, 0, unroll=3)
    for load in loads[4:]:
        load.wait()
    drain(reports_ref, devices - 1, report_send_sem)
    drain(reports_ref, devices - 1, report_recv_sem)

    @pl.when(is_home)
    def _():
        start, size = group_rows(size_ref, lanes, groups)
        amount = size.astype(jnp.float32) * cols
        lane = lax.broadcasted_iota(jnp.int32, (1, lanes), 1)
        seen = []
        for band in range(bands):
            report = reports_ref[band * pieces : (band + 1) * pieces, 0]
            centre = jnp.sum(report, axis=0, keepdims=True) / pieces
            offset = report - centre
            between = amount * jnp.sum(offset * offset, axis=0, keepdims=True)
            within = jnp.sum(report, axis=0, keepdims=True)
            seen.append((report, centre, between, within))
        band_of = []
        for band in range(bands):
            for row in range(rows):
                mark = lane == 2 * rows * groups + row
                number = jnp.sum(jnp.where(mark, seen[band][0][:1], 0.0)).astype(jnp.int32)
                band_of.append(jnp.clip(number, 0, band_count - 1))
        for part in range(parts):
            pltpu.make_async_copy(
                flat_ref.at[pl.ds(0, SUB)], arrived_ref.at[part, me], local_sem.at[part]
            ).wait()
            drain(arrived_ref.at[part], devices - 1, block_recv_sem.at[part])
            member = membership(own_home * chan + part * SUB, SUB, start, size)
            for band in range(bands):
                for piece in range(pieces):
                    cells = arrived_ref[part, band * pieces + piece].astype(jnp.float32)
                    for row in range(rows):
                        at = (band * rows + row) * SUB
                        wide_ref[at : at + SUB, piece * cols : (piece + 1) * cols] = cells[
                            :, row * cols : (row + 1) * cols
                        ]
            raw = jnp.dot(
                wide_ref[...].astype(jnp.bfloat16), table_ref[...],
                preferred_element_type=jnp.float32,
            )
            for band in range(bands):
                _, centre, between, within = seen[band]
                for row in range(rows):
                    low, high = row * groups, (rows + row) * groups
                    here = member & (lane >= low) & (lane < low + groups)
                    there = member & (lane >= high) & (lane < high + groups)

                    def pick(mask, cells):
                        return jnp.sum(jnp.where(mask, cells, 0.0), axis=1, keepdims=True)

                    square = pick(here, between) + pick(there, within)
                    count = pick(here, amount) * pieces
                    mean = pick(here, centre)
                    scale = lax.rsqrt(square / jnp.maximum(count, 1.0) + EPSILON)
                    at = (band * rows + row) * SUB
                    spec_ref[at : at + SUB] = (raw[at : at + SUB] - mean * total_ref[...]) * scale
            for row in range(lat):
                real = jnp.zeros((SUB, bins), jnp.float32)
                imag = jnp.zeros((SUB, bins), jnp.float32)
                for tap in range(TAPS):
                    source = row + tap - HALO
                    if source < 0 or source >= lat:
                        continue
                    at = source * SUB
                    spec_real = spec_ref[at : at + SUB, :bins]
                    spec_imag = spec_ref[at : at + SUB, bins:]
                    index = band_of[row] * TAPS + tap
                    at = part * SUB
                    kern_real = kern_ref[index, at : at + SUB]
                    kern_imag = kern_ref[index, chan + at : chan + at + SUB]
                    real = real + kern_real * spec_real - kern_imag * spec_imag
                    imag = imag + kern_real * spec_imag + kern_imag * spec_real
                prod_ref[row * SUB : (row + 1) * SUB, :bins] = real
                prod_ref[row * SUB : (row + 1) * SUB, bins:] = imag
            corr_ref[...] = lax.dot_general(
                (prod_ref[...] * weight_ref[...]).astype(jnp.bfloat16),
                table_ref[...],
                OVER_LAST,
                preferred_element_type=jnp.float32,
            )
            for band in range(bands):
                for piece in range(pieces):
                    pieces_of = []
                    for row in range(rows):
                        at = (band * rows + row) * SUB
                        pieces_of.append(
                            corr_ref[at : at + SUB, piece * cols : (piece + 1) * cols]
                        )
                    device = band * pieces + piece
                    cells = arrived_ref[part, device].astype(jnp.float32)
                    mixed_ref[part, device] = (
                        cells + jnp.concatenate(pieces_of, axis=1)
                    ).astype(jnp.bfloat16)
            first = pl.multiple_of(own_home * chan + part * SUB, SUB)

            def give(step, carry):
                target = lax.rem(me + step, devices)
                pltpu.make_async_remote_copy(
                    src_ref=mixed_ref.at[part, target],
                    dst_ref=returned_ref.at[pl.ds(first, SUB)],
                    send_sem=mixed_send_sem,
                    recv_sem=mixed_recv_sem,
                    device_id=place(target),
                    device_id_type=MESH,
                ).start()
                return carry

            lax.fori_loop(1, devices, give, 0)
            pltpu.make_async_copy(
                mixed_ref.at[part, me], returned_ref.at[pl.ds(first, SUB)], local_sem.at[part]
            ).start()
        for part in range(parts):
            pltpu.make_async_copy(
                mixed_ref.at[part, me], returned_ref.at[pl.ds(0, SUB)], local_sem.at[part]
            ).wait()
            drain(mixed_ref.at[part], devices - 1, mixed_send_sem)
        drain(flat_ref, (homes - 1) * chan, block_send_sem)
        drain(returned_ref, (homes - 1) * chan, mixed_recv_sem)

    @pl.when(jnp.logical_not(is_home))
    def _():
        drain(flat_ref, homes * chan, block_send_sem)
        drain(returned_ref, homes * chan, mixed_recv_sem)

    step = pixels // 3 if pixels % 24 == 0 else pixels
    for at in range(0, pixels, step):
        inputs = lax.dot_general(
            order_ref[at : at + step, :], returned_ref[...], OVER_LAST,
            preferred_element_type=jnp.float32,
        )[:, :chan_count]
        centre = jnp.mean(inputs, axis=-1, keepdims=True)
        spread = jnp.mean((inputs - centre) ** 2, axis=-1, keepdims=True)
        normalised = (
            (inputs - centre) * lax.rsqrt(spread + EPSILON) * gain_ref[...]
        ).astype(jnp.bfloat16)
        hidden = jnp.dot(normalised, win_ref[...], preferred_element_type=jnp.float32)
        hidden = (0.5 * hidden * (1.0 + lax.erf(hidden * math.sqrt(0.5)))).astype(jnp.bfloat16)
        result = inputs + lax.dot_general(
            hidden, wout_ref[...], OVER_LAST, preferred_element_type=jnp.float32
        )
        out_ref[at : at + step] = result.astype(jnp.bfloat16)


def per_device(fields, group_size, band_of_row, basis_spectra, basis_coef, mlp_gain, w_in, w_out):
    row_count, col_count, chan_count = fields.shape
    pieces = lax.axis_size("lon")
    bands = lax.axis_size("lat")
    devices = pieces * bands
    lon_count = col_count * pieces
    lat_count = row_count * bands
    freq_count = lon_count // 2 + 1
    groups = group_size.shape[0]
    pixels = row_count * col_count
    chan = round_up(-(-chan_count // devices), SUB)
    homes = -(-chan_count // chan)
    parts = chan // SUB
    bins = round_up(freq_count, 128)
    band_count, _, basis_count = basis_spectra.shape[:3]
    hidden = w_in.shape[1]
    lanes = round_up((2 * groups + 1) * row_count, 128)
    table, total, weight = dft_tables(lon_count, bins)
    basis = basis_spectra.reshape(band_count * TAPS, basis_count, 2, freq_count)
    f32, bf16 = jnp.float32, jnp.bfloat16
    operands = [
        (jnp.transpose(fields, (1, 0, 2)), bf16),
        (pixel_order(row_count, col_count), bf16),
        (basis_coef.T, f32),
        (basis, f32),
        (table, bf16),
        (total, f32),
        (weight, f32),
        (mlp_gain.reshape(1, chan_count), f32),
        (w_in, bf16),
        (w_out.T, bf16),
    ]
    out = pl.pallas_call(
        functools.partial(
            block_body, devices, homes, chan, freq_count, bins, row_count, col_count,
            chan_count, groups,
        ),
        out_shape=jax.ShapeDtypeStruct((pixels, chan_count), bf16),
        in_specs=[SMEM] * 2 + [ANY] * len(operands),
        out_specs=VMEM,
        scratch_shapes=[pltpu.VMEM(array.shape, kind) for array, kind in operands]
        + [
            pltpu.VMEM((homes * chan, pixels), bf16),
            pltpu.VMEM((parts, devices, SUB, pixels), bf16),
            pltpu.VMEM((parts, devices, SUB, pixels), bf16),
            pltpu.VMEM((homes * chan, pixels), bf16),
            pltpu.VMEM((1, lanes), f32),
            pltpu.VMEM((devices, 1, lanes), f32),
            pltpu.VMEM((band_count * TAPS, 2 * chan, bins), f32),
            pltpu.VMEM((lat_count * SUB, lon_count), f32),
            pltpu.VMEM((lat_count * SUB, 2 * bins), f32),
            pltpu.VMEM((lat_count * SUB, 2 * bins), f32),
            pltpu.VMEM((lat_count * SUB, lon_count), f32),
            DMA((len(operands),)),
            DMA,
            DMA((parts,)),
            DMA,
            DMA,
            DMA,
            DMA,
            DMA((parts,)),
        ],
        compiler_params=pltpu.CompilerParams(
            collective_id=0, has_side_effects=True, vmem_limit_bytes=60 * 1024 * 1024
        ),
    )(group_size, band_of_row, *[array for array, _ in operands])
    return jnp.transpose(out.reshape(col_count, row_count, chan_count), (1, 0, 2))


def solution(mesh):
    placed = (P("lat", "lon", None), P(), P("lat"), P(), P(), P(), P(), P())
    return jax.shard_map(
        per_device, mesh=mesh, in_specs=placed, out_specs=P("lat", "lon", None), check_vma=False
    )
```

time: 69.1 us -> 45.9 us (0.66)
  Pallas kernels: 52.4 us -> 42.2 us
  matrix products: 8.08 us -> 0 us
  other arithmetic: 2.38 us -> 0 us
  local copies, waits for them, and re-layouts: 5.84 us -> 3.52 us
    pallas_call x3 -> x1, Pallas kernels: 52.4 us -> 42.2 us  [per_device(): pl.pallas_call(functools.partial(block_body, devices, homes, chan, freq_c...]
    dot_general x1 -> x0, matrix products: 8.08 us -> none  [per_device(): result = inputs + jnp.dot(hidden, w_out, preferred_element_type=jnp.float32)]
    reduce_sum x2 -> x0, other arithmetic: 2.37 us -> none  [the longest x1 1.21 us: per_device(): spread = jnp.mean((inputs - centre) ** 2, axis=-1, keepdims=True)]
    reshape x4 -> x2, local copies, waits for them, and re-layouts: 4.99 us -> 3.52 us  [the longest x1 2.25 us: per_device(): out.reshape(col_count, row_count, chan_count)]
    pad x1 -> x0, local copies, waits for them, and re-layouts: 0.84 us -> none  [per_device(): turned = jnp.pad(turned, ((0, active * chan - chan_count), (0, 0)))]
where the time goes in v1:
time: 45.9 us; the launch traced here: 45.7 us
  Pallas kernels  42.2 us (92%)
  local copies, waits for them, and re-layouts  3.52 us (8%)
    pallas_call x1, Pallas kernels, per_device(): pl.pallas_call(functools.partial(block_body, devices, homes, chan, freq_c...  42.2 us
    reshape x1, local copies, waits for them, and re-layouts, per_device(): out.reshape(col_count, row_count, chan_count)  2.25 us
    reshape x1, local copies, waits for them, and re-layouts, per_device(): mlp_gain.reshape(1, chan_count)  1.27 us

profile of v1, /device:TPU:0, one launch (start us, length us, event | category | flops | bytes accessed | tf_op | source)
XLA Modules:
  0.0 45.7 jit_solution(3028231286677773005)
XLA Ops:
  0.0 1.3 %reshape.10.gain_hbm = f32[1,641]{1,0:T(1,128)} reshape(f32[641]{0:T(1024)} %param.17) | data formatting | bytes 5128 | tf_op jit(solution)/shard_map/reshape | solution.py:432
  1.3 42.2 %shard_map.118 = bf16[360,641]{1,0:T(8,128)(2,1)} custom-call(s32[8]{0:T(128)} %size_ref.1, s32[4]{0:T(128)} %band_ref.1, bf16[90,4,641]{2,1,0:T(4,128)(2,1)} %bitcast.7, bf16[360,360]{1,0:T(8,128)(2,1)} %constant.8.clone.order_hbm, f32[8,641]{1,0:T(8,128)} %bitcast.8, f32[72,8,2,361]{3,2,1,0:T(2,128)} %bitcast.6, bf16[720,768]{1,0:T(8,128)(2,1)} %constant.9.clone.table_hbm, ...), custom_call_target="tpu_custom_call" | custom-call | tf_op jit(solution)/shard_map/pallas_call | solution.py:436
  43.5 2.3 %reshape.11 = bf16[90,4,641]{2,1,0:T(4,128)(2,1)} reshape(bf16[360,641]{1,0:T(8,128)(2,1)} %shard_map.118) | data formatting | bytes 923040 | tf_op jit(solution)/shard_map/reshape | solution.py:470

commit v2 on v1

--- a/solution.py
+++ b/solution.py
@@ -15,7 +15,7 @@
 SUB = 8
 VMEM = pl.BlockSpec(memory_space=pltpu.VMEM)
 SMEM = pl.BlockSpec(memory_space=pltpu.SMEM)
-ANY = pl.BlockSpec(memory_space=pl.ANY)
+HBM = pl.BlockSpec(memory_space=pltpu.HBM)
 MESH = pl.DeviceIdType.MESH
 DMA = pltpu.SemaphoreType.DMA
 
@@ -217,9 +217,6 @@
     report_ref[...] = report
     reports_ref[me] = report
 
-    for part in range(1, parts):
-        send_part(part)
-
     def tell(step, carry):
         pltpu.make_async_remote_copy(
             src_ref=report_ref,
@@ -232,6 +229,8 @@
         return carry
 
     lax.fori_loop(1, devices, tell, 0)
+    for part in range(1, parts):
+        send_part(part)
 
     loads[2].wait()
     loads[3].wait()
@@ -382,7 +381,7 @@
         drain(flat_ref, homes * chan, block_send_sem)
         drain(returned_ref, homes * chan, mixed_recv_sem)
 
-    step = pixels // 3 if pixels % 24 == 0 else pixels
+    step = pixels
     for at in range(0, pixels, step):
         inputs = lax.dot_general(
             order_ref[at : at + step, :], returned_ref[...], OVER_LAST,
@@ -391,14 +390,16 @@
         centre = jnp.mean(inputs, axis=-1, keepdims=True)
         spread = jnp.mean((inputs - centre) ** 2, axis=-1, keepdims=True)
         normalised = (
-            (inputs - centre) * lax.rsqrt(spread + EPSILON) * gain_ref[...]
+            (inputs - centre) * lax.rsqrt(spread + EPSILON) * gain_ref[...].reshape(1, chan_count)
         ).astype(jnp.bfloat16)
         hidden = jnp.dot(normalised, win_ref[...], preferred_element_type=jnp.float32)
         hidden = (0.5 * hidden * (1.0 + lax.erf(hidden * math.sqrt(0.5)))).astype(jnp.bfloat16)
         result = inputs + lax.dot_general(
             hidden, wout_ref[...], OVER_LAST, preferred_element_type=jnp.float32
         )
-        out_ref[at : at + step] = result.astype(jnp.bfloat16)
+        out_ref[at // rows : (at + step) // rows] = result.astype(jnp.bfloat16).reshape(
+            step // rows, rows, chan_count
+        )
 
 
 def per_device(fields, group_size, band_of_row, basis_spectra, basis_coef, mlp_gain, w_in, w_out):
@@ -429,7 +430,7 @@
         (table, bf16),
         (total, f32),
         (weight, f32),
-        (mlp_gain.reshape(1, chan_count), f32),
+        (mlp_gain, f32),
         (w_in, bf16),
         (w_out.T, bf16),
     ]
@@ -438,8 +439,8 @@
             block_body, devices, homes, chan, freq_count, bins, row_count, col_count,
             chan_count, groups,
         ),
-        out_shape=jax.ShapeDtypeStruct((pixels, chan_count), bf16),
-        in_specs=[SMEM] * 2 + [ANY] * len(operands),
+        out_shape=jax.ShapeDtypeStruct((col_count, row_count, chan_count), bf16),
+        in_specs=[SMEM] * 2 + [HBM] * len(operands),
         out_specs=VMEM,
         scratch_shapes=[pltpu.VMEM(array.shape, kind) for array, kind in operands]
         + [
@@ -467,7 +468,7 @@
             collective_id=0, has_side_effects=True, vmem_limit_bytes=60 * 1024 * 1024
         ),
     )(group_size, band_of_row, *[array for array, _ in operands])
-    return jnp.transpose(out.reshape(col_count, row_count, chan_count), (1, 0, 2))
+    return jnp.transpose(out, (1, 0, 2))
 
 
 def solution(mesh):

time: 45.9 us -> 38.8 us (0.85)
  Pallas kernels: 42.2 us -> 36.6 us
  local copies, waits for them, and re-layouts: 3.52 us -> 2.05 us
    pallas_call x1, Pallas kernels: 42.2 us -> 36.6 us  [per_device(): pl.pallas_call(functools.partial(block_body, devices, homes, chan, freq_c...]
    reshape x2 -> x0, local copies, waits for them, and re-layouts: 3.52 us -> none  [the longest x1 2.25 us: per_device(): out.reshape(col_count, row_count, chan_count)]
    unnamed x0 -> x1, local copies, waits for them, and re-layouts: none -> 2.05 us
where the time goes in v2:
time: 38.8 us; the launch traced here: 38.6 us
  Pallas kernels  36.6 us (94%)
  local copies, waits for them, and re-layouts  2.05 us (5%)
    pallas_call x1, Pallas kernels, per_device(): pl.pallas_call(functools.partial(block_body, devices, homes, chan, freq_c...  36.6 us
    unnamed x1, local copies, waits for them, and re-layouts  2.05 us

profile of v2, /device:TPU:0, one launch (start us, length us, event | category | flops | bytes accessed | tf_op | source)
XLA Modules:
  0.0 38.6 jit_solution(15034757166072359261)
XLA Ops:
  0.0 36.6 %shard_map.118 = bf16[90,4,641]{2,1,0:T(4,128)(2,1)} custom-call(s32[8]{0:T(128)} %size_ref.1, s32[4]{0:T(128)} %band_ref.1, bf16[90,4,641]{2,1,0:T(4,128)(2,1)} %bitcast.8, bf16[360,360]{1,0:T(8,128)(2,1)} %constant.8.clone.order_hbm, f32[8,641]{1,0:T(8,128)} %bitcast.9, f32[72,8,2,361]{3,2,1,0:T(2,128)} %bitcast.7, ...), custom_call_target="tpu_custom_call" | custom-call | tf_op jit(solution)/shard_map/pallas_call | solution.py:437
  36.6 2.0 %copy.14 = bf16[4,90,641]{2,0,1:T(4,128)(2,1)} copy(bf16[4,90,641]{2,0,1:T(4,128)(2,1)} %bitcast.5) | data formatting | bytes 923040

commit v3 on v2

--- a/solution.py
+++ b/solution.py
@@ -14,7 +14,6 @@
 EPSILON = 1e-05
 SUB = 8
 VMEM = pl.BlockSpec(memory_space=pltpu.VMEM)
-SMEM = pl.BlockSpec(memory_space=pltpu.SMEM)
 HBM = pl.BlockSpec(memory_space=pltpu.HBM)
 MESH = pl.DeviceIdType.MESH
 DMA = pltpu.SemaphoreType.DMA
@@ -87,23 +86,25 @@
 
 
 def block_body(
-    devices, homes, chan, freq, bins, rows, cols, chan_count, groups,
-    size_ref, band_ref,
-    x_hbm, order_hbm, coef_hbm, basis_hbm, table_hbm, total_hbm, weight_hbm, gain_hbm,
+    devices, homes, sizes, freq, bins, rows, cols, chan_count, groups,
+    size_hbm, band_hbm, x_hbm, order_hbm, coef_hbm, basis_hbm, table_hbm, total_hbm, weight_hbm, gain_hbm,
     win_hbm, wout_hbm,
     out_ref,
-    x_ref, order_ref, coef_ref, basis_ref, table_ref, total_ref, weight_ref, gain_ref,
+    size_ref, band_ref, x_ref, order_ref, coef_ref, basis_ref, table_ref, total_ref, weight_ref, gain_ref,
     win_ref, wout_ref,
-    flat_ref, arrived_ref, mixed_ref, returned_ref, report_ref, reports_ref,
+    flat_ref, returned_ref, report_ref, reports_ref,
     kern_ref, wide_ref, spec_ref, prod_ref, corr_ref,
     load_sem, block_send_sem, block_recv_sem, report_send_sem, report_recv_sem,
-    mixed_send_sem, mixed_recv_sem, local_sem,
+    mixed_send_sem, mixed_recv_sem, local_sem, *part_refs,
 ):
     me = own_index()
     pieces = lax.axis_size("lon")
     bands = devices // pieces
     lat = bands * rows
-    parts = chan // SUB
+    parts = len(sizes)
+    chan = sum(sizes)
+    offsets = [sum(sizes[:part]) for part in range(parts)]
+    arrived_refs, mixed_refs = part_refs[:parts], part_refs[parts:]
     pixels = rows * cols
     band_count = basis_ref.shape[0] // TAPS
     own_home = lax.div(me * homes + devices - 1, devices)
@@ -113,28 +114,31 @@
     def device_of(home):
         return lax.div(home * devices, homes)
 
+    barrier = pltpu.get_barrier_semaphore()
+
+    def greet(step, carry):
+        pl.semaphore_signal(
+            barrier, inc=1, device_id=place(lax.rem(me + step, devices)), device_id_type=MESH
+        )
+        return carry
+
     loads = [
         pltpu.make_async_copy(source, target, load_sem.at[index])
         for index, (source, target) in enumerate(
             [
-                (x_hbm, x_ref), (order_hbm, order_ref), (coef_hbm, coef_ref),
+                (x_hbm, x_ref), (order_hbm, order_ref), (size_hbm, size_ref),
+                (band_hbm, band_ref), (coef_hbm, coef_ref),
                 (basis_hbm, basis_ref), (table_hbm, table_ref), (total_hbm, total_ref),
                 (weight_hbm, weight_ref), (gain_hbm, gain_ref), (win_hbm, win_ref),
                 (wout_hbm, wout_ref),
             ]
         )
     ]
-    for load in loads:
+    for load in loads[:2]:
         load.start()
-    barrier = pltpu.get_barrier_semaphore()
-
-    def greet(step, carry):
-        pl.semaphore_signal(
-            barrier, inc=1, device_id=place(lax.rem(me + step, devices)), device_id_type=MESH
-        )
-        return carry
-
     lax.fori_loop(1, devices, greet, 0)
+    for load in loads[2:]:
+        load.start()
     loads[0].wait()
     loads[1].wait()
     x = x_ref[...].reshape(pixels, chan_count)
@@ -149,12 +153,13 @@
         def send(step, carry):
             home = lax.rem(own_home + step, homes)
             target = device_of(home)
+            first = pl.multiple_of(home * chan + offsets[part], SUB)
 
             @pl.when(target != me)
             def _():
                 pltpu.make_async_remote_copy(
-                    src_ref=flat_ref.at[pl.ds(pl.multiple_of(home * chan + part * SUB, SUB), SUB)],
-                    dst_ref=arrived_ref.at[part, me],
+                    src_ref=flat_ref.at[pl.ds(first, sizes[part])],
+                    dst_ref=arrived_refs[part].at[me],
                     send_sem=block_send_sem,
                     recv_sem=block_recv_sem.at[part],
                     device_id=place(target),
@@ -170,11 +175,14 @@
     @pl.when(is_home)
     def _():
         for part in range(parts):
-            first = pl.multiple_of(own_home * chan + part * SUB, SUB)
+            first = pl.multiple_of(own_home * chan + offsets[part], SUB)
             pltpu.make_async_copy(
-                flat_ref.at[pl.ds(first, SUB)], arrived_ref.at[part, me], local_sem.at[part]
+                flat_ref.at[pl.ds(first, sizes[part])], arrived_refs[part].at[me],
+                local_sem.at[part],
             ).start()
 
+    loads[2].wait()
+    loads[3].wait()
     lane = lax.broadcasted_iota(jnp.int32, (pixels, 128), 0)
     slot = lax.broadcasted_iota(jnp.int32, (pixels, 128), 1)
     segment = (lane >= slot * cols) & (lane < (slot + 1) * cols)
@@ -232,8 +240,8 @@
     for part in range(1, parts):
         send_part(part)
 
-    loads[2].wait()
-    loads[3].wait()
+    loads[4].wait()
+    loads[5].wait()
     wanted = own_home * chan + lax.broadcasted_iota(jnp.int32, (chan, chan_count), 0)
     chosen = jnp.where(
         lax.broadcasted_iota(jnp.int32, (chan, chan_count), 1) == wanted, 1.0, 0.0
@@ -255,7 +263,7 @@
         return carry
 
     lax.fori_loop(0, basis_ref.shape[0], generate, 0, unroll=3)
-    for load in loads[4:]:
+    for load in loads[6:]:
         load.wait()
     drain(reports_ref, devices - 1, report_send_sem)
     drain(reports_ref, devices - 1, report_recv_sem)
@@ -280,21 +288,23 @@
                 number = jnp.sum(jnp.where(mark, seen[band][0][:1], 0.0)).astype(jnp.int32)
                 band_of.append(jnp.clip(number, 0, band_count - 1))
         for part in range(parts):
+            size_of, arrived_ref, mixed_ref = sizes[part], arrived_refs[part], mixed_refs[part]
+            span = lat * size_of
             pltpu.make_async_copy(
-                flat_ref.at[pl.ds(0, SUB)], arrived_ref.at[part, me], local_sem.at[part]
+                flat_ref.at[pl.ds(0, size_of)], arrived_ref.at[me], local_sem.at[part]
             ).wait()
-            drain(arrived_ref.at[part], devices - 1, block_recv_sem.at[part])
-            member = membership(own_home * chan + part * SUB, SUB, start, size)
+            drain(arrived_ref, devices - 1, block_recv_sem.at[part])
+            member = membership(own_home * chan + offsets[part], size_of, start, size)
             for band in range(bands):
                 for piece in range(pieces):
-                    cells = arrived_ref[part, band * pieces + piece].astype(jnp.float32)
+                    cells = arrived_ref[band * pieces + piece].astype(jnp.float32)
                     for row in range(rows):
-                        at = (band * rows + row) * SUB
-                        wide_ref[at : at + SUB, piece * cols : (piece + 1) * cols] = cells[
+                        at = (band * rows + row) * size_of
+                        wide_ref[at : at + size_of, piece * cols : (piece + 1) * cols] = cells[
                             :, row * cols : (row + 1) * cols
                         ]
             raw = jnp.dot(
-                wide_ref[...].astype(jnp.bfloat16), table_ref[...],
+                wide_ref[:span].astype(jnp.bfloat16), table_ref[...],
                 preferred_element_type=jnp.float32,
             )
             for band in range(bands):
@@ -311,28 +321,28 @@
                     count = pick(here, amount) * pieces
                     mean = pick(here, centre)
                     scale = lax.rsqrt(square / jnp.maximum(count, 1.0) + EPSILON)
-                    at = (band * rows + row) * SUB
-                    spec_ref[at : at + SUB] = (raw[at : at + SUB] - mean * total_ref[...]) * scale
+                    at = (band * rows + row) * size_of
+                    spec_ref[at : at + size_of] = (raw[at : at + size_of] - mean * total_ref[...]) * scale
             for row in range(lat):
-                real = jnp.zeros((SUB, bins), jnp.float32)
-                imag = jnp.zeros((SUB, bins), jnp.float32)
+                real = jnp.zeros((size_of, bins), jnp.float32)
+                imag = jnp.zeros((size_of, bins), jnp.float32)
                 for tap in range(TAPS):
                     source = row + tap - HALO
                     if source < 0 or source >= lat:
                         continue
-                    at = source * SUB
-                    spec_real = spec_ref[at : at + SUB, :bins]
-                    spec_imag = spec_ref[at : at + SUB, bins:]
+                    at = source * size_of
+                    spec_real = spec_ref[at : at + size_of, :bins]
+                    spec_imag = spec_ref[at : at + size_of, bins:]
                     index = band_of[row] * TAPS + tap
-                    at = part * SUB
-                    kern_real = kern_ref[index, at : at + SUB]
-                    kern_imag = kern_ref[index, chan + at : chan + at + SUB]
+                    at = offsets[part]
+                    kern_real = kern_ref[index, at : at + size_of]
+                    kern_imag = kern_ref[index, chan + at : chan + at + size_of]
                     real = real + kern_real * spec_real - kern_imag * spec_imag
                     imag = imag + kern_real * spec_imag + kern_imag * spec_real
-                prod_ref[row * SUB : (row + 1) * SUB, :bins] = real
-                prod_ref[row * SUB : (row + 1) * SUB, bins:] = imag
-            corr_ref[...] = lax.dot_general(
-                (prod_ref[...] * weight_ref[...]).astype(jnp.bfloat16),
+                prod_ref[row * size_of : (row + 1) * size_of, :bins] = real
+                prod_ref[row * size_of : (row + 1) * size_of, bins:] = imag
+            corr_ref[:span] = lax.dot_general(
+                (prod_ref[:span] * weight_ref[...]).astype(jnp.bfloat16),
                 table_ref[...],
                 OVER_LAST,
                 preferred_element_type=jnp.float32,
@@ -341,38 +351,43 @@
                 for piece in range(pieces):
                     pieces_of = []
                     for row in range(rows):
-                        at = (band * rows + row) * SUB
+                        at = (band * rows + row) * size_of
                         pieces_of.append(
-                            corr_ref[at : at + SUB, piece * cols : (piece + 1) * cols]
+                            corr_ref[at : at + size_of, piece * cols : (piece + 1) * cols]
                         )
                     device = band * pieces + piece
-                    cells = arrived_ref[part, device].astype(jnp.float32)
-                    mixed_ref[part, device] = (
+                    cells = arrived_ref[device].astype(jnp.float32)
+                    mixed_ref[device] = (
                         cells + jnp.concatenate(pieces_of, axis=1)
                     ).astype(jnp.bfloat16)
-            first = pl.multiple_of(own_home * chan + part * SUB, SUB)
+            first = pl.multiple_of(own_home * chan + offsets[part], SUB)
 
             def give(step, carry):
-                target = lax.rem(me + step, devices)
-                pltpu.make_async_remote_copy(
-                    src_ref=mixed_ref.at[part, target],
-                    dst_ref=returned_ref.at[pl.ds(first, SUB)],
-                    send_sem=mixed_send_sem,
-                    recv_sem=mixed_recv_sem,
-                    device_id=place(target),
-                    device_id_type=MESH,
-                ).start()
+                target = step
+
+                @pl.when(target != me)
+                def _():
+                    pltpu.make_async_remote_copy(
+                        src_ref=mixed_ref.at[target],
+                        dst_ref=returned_ref.at[pl.ds(first, size_of)],
+                        send_sem=mixed_send_sem,
+                        recv_sem=mixed_recv_sem,
+                        device_id=place(target),
+                        device_id_type=MESH,
+                    ).start()
+
                 return carry
 
-            lax.fori_loop(1, devices, give, 0)
+            lax.fori_loop(0, devices, give, 0)
             pltpu.make_async_copy(
-                mixed_ref.at[part, me], returned_ref.at[pl.ds(first, SUB)], local_sem.at[part]
+                mixed_ref.at[me], returned_ref.at[pl.ds(first, size_of)], local_sem.at[part]
             ).start()
         for part in range(parts):
             pltpu.make_async_copy(
-                mixed_ref.at[part, me], returned_ref.at[pl.ds(0, SUB)], local_sem.at[part]
+                mixed_refs[part].at[me], returned_ref.at[pl.ds(0, sizes[part])],
+                local_sem.at[part],
             ).wait()
-            drain(mixed_ref.at[part], devices - 1, mixed_send_sem)
+            drain(mixed_refs[part], devices - 1, mixed_send_sem)
         drain(flat_ref, (homes - 1) * chan, block_send_sem)
         drain(returned_ref, (homes - 1) * chan, mixed_recv_sem)
 
@@ -414,7 +429,9 @@
     pixels = row_count * col_count
     chan = round_up(-(-chan_count // devices), SUB)
     homes = -(-chan_count // chan)
-    parts = chan // SUB
+    sizes = [SUB] + [chan - SUB] * (chan > SUB)
+    parts = len(sizes)
+    tallest = lat_count * max(sizes)
     bins = round_up(freq_count, 128)
     band_count, _, basis_count = basis_spectra.shape[:3]
     hidden = w_in.shape[1]
@@ -422,6 +439,7 @@
     table, total, weight = dft_tables(lon_count, bins)
     basis = basis_spectra.reshape(band_count * TAPS, basis_count, 2, freq_count)
     f32, bf16 = jnp.float32, jnp.bfloat16
+    scalars = [group_size, band_of_row]
     operands = [
         (jnp.transpose(fields, (1, 0, 2)), bf16),
         (pixel_order(row_count, col_count), bf16),
@@ -436,26 +454,25 @@
     ]
     out = pl.pallas_call(
         functools.partial(
-            block_body, devices, homes, chan, freq_count, bins, row_count, col_count,
+            block_body, devices, homes, sizes, freq_count, bins, row_count, col_count,
             chan_count, groups,
         ),
         out_shape=jax.ShapeDtypeStruct((col_count, row_count, chan_count), bf16),
-        in_specs=[SMEM] * 2 + [HBM] * len(operands),
+        in_specs=[HBM] * (len(scalars) + len(operands)),
         out_specs=VMEM,
-        scratch_shapes=[pltpu.VMEM(array.shape, kind) for array, kind in operands]
+        scratch_shapes=[pltpu.SMEM(array.shape, jnp.int32) for array in scalars]
+        + [pltpu.VMEM(array.shape, kind) for array, kind in operands]
         + [
             pltpu.VMEM((homes * chan, pixels), bf16),
-            pltpu.VMEM((parts, devices, SUB, pixels), bf16),
-            pltpu.VMEM((parts, devices, SUB, pixels), bf16),
             pltpu.VMEM((homes * chan, pixels), bf16),
             pltpu.VMEM((1, lanes), f32),
             pltpu.VMEM((devices, 1, lanes), f32),
             pltpu.VMEM((band_count * TAPS, 2 * chan, bins), f32),
-            pltpu.VMEM((lat_count * SUB, lon_count), f32),
-            pltpu.VMEM((lat_count * SUB, 2 * bins), f32),
-            pltpu.VMEM((lat_count * SUB, 2 * bins), f32),
-            pltpu.VMEM((lat_count * SUB, lon_count), f32),
-            DMA((len(operands),)),
+            pltpu.VMEM((tallest, lon_count), f32),
+            pltpu.VMEM((tallest, 2 * bins), f32),
+            pltpu.VMEM((tallest, 2 * bins), f32),
+            pltpu.VMEM((tallest, lon_count), f32),
+            DMA((len(scalars) + len(operands),)),
             DMA,
             DMA((parts,)),
             DMA,
@@ -463,11 +480,12 @@
             DMA,
             DMA,
             DMA((parts,)),
-        ],
+        ]
+        + [pltpu.VMEM((devices, size, pixels), bf16) for size in sizes] * 2,
         compiler_params=pltpu.CompilerParams(
             collective_id=0, has_side_effects=True, vmem_limit_bytes=60 * 1024 * 1024
         ),
-    )(group_size, band_of_row, *[array for array, _ in operands])
+    )(*scalars, *[array for array, _ in operands])
     return jnp.transpose(out, (1, 0, 2))
 
 

time: 38.8 us -> 37.3 us (0.961)
  the two profiles are of different devices: /device:TPU:0 before, /device:TPU:31 now
where the time goes in v3:
time: 37.3 us; the launch traced here: 37.2 us
  Pallas kernels  35.2 us (94%)
  local copies, waits for them, and re-layouts  2.05 us (5%)
    pallas_call x1, Pallas kernels, per_device(): pl.pallas_call(functools.partial(block_body, devices, homes, sizes, freq_...  35.2 us
    unnamed x1, local copies, waits for them, and re-layouts  2.05 us

profile of v3, /device:TPU:31, one launch (start us, length us, event | category | flops | bytes accessed | tf_op | source)
XLA Modules:
  0.0 37.2 jit_solution(4488866866506340409)
XLA Ops:
  0.0 35.2 %shard_map.118 = bf16[90,4,641]{2,1,0:T(4,128)(2,1)} custom-call(s32[8]{0:T(128)} %size_hbm.1, s32[4]{0:T(128)} %band_hbm.1, bf16[90,4,641]{2,1,0:T(4,128)(2,1)} %bitcast.8, bf16[360,360]{1,0:T(8,128)(2,1)} %constant.8.clone.order_hbm, f32[8,641]{1,0:T(8,128)} %bitcast.9, f32[72,8,2,361]{3,2,1,0:T(2,128)} %bitcast.7, ...), custom_call_target="tpu_custom_call" | custom-call | tf_op jit(solution)/shard_map/pallas_call | solution.py:455
  35.2 2.0 %copy.14 = bf16[4,90,641]{2,0,1:T(4,128)(2,1)} copy(bf16[4,90,641]{2,0,1:T(4,128)(2,1)} %bitcast.5) | data formatting | bytes 923040

commit v4 on v3

--- a/solution.py
+++ b/solution.py
@@ -93,7 +93,7 @@
     size_ref, band_ref, x_ref, order_ref, coef_ref, basis_ref, table_ref, total_ref, weight_ref, gain_ref,
     win_ref, wout_ref,
     flat_ref, returned_ref, report_ref, reports_ref,
-    kern_ref, wide_ref, spec_ref, prod_ref, corr_ref,
+    kern_ref, wide_ref, spec_ref, prod_ref, corr_ref, rest_ref,
     load_sem, block_send_sem, block_recv_sem, report_send_sem, report_recv_sem,
     mixed_send_sem, mixed_recv_sem, local_sem, *part_refs,
 ):
@@ -265,6 +265,14 @@
     lax.fori_loop(0, basis_ref.shape[0], generate, 0, unroll=3)
     for load in loads[6:]:
         load.wait()
+    rest = win_ref.shape[1] % 256
+    rest = rest if rest <= SUB else 0
+    whole = win_ref.shape[1] - rest
+    if rest:
+        for index, weights in enumerate((win_ref, wout_ref)):
+            tail = weights[:, whole:].astype(jnp.float32)
+            tail = jnp.concatenate([tail, jnp.zeros((chan_count, 128 - rest), jnp.float32)], axis=1)
+            rest_ref[index * SUB : (index + 1) * SUB] = tail.T[:SUB]
     drain(reports_ref, devices - 1, report_send_sem)
     drain(reports_ref, devices - 1, report_recv_sem)
 
@@ -396,6 +404,9 @@
         drain(flat_ref, homes * chan, block_send_sem)
         drain(returned_ref, homes * chan, mixed_recv_sem)
 
+    def gelu(hidden):
+        return (0.5 * hidden * (1.0 + lax.erf(hidden * math.sqrt(0.5)))).astype(jnp.bfloat16)
+
     step = pixels
     for at in range(0, pixels, step):
         inputs = lax.dot_general(
@@ -407,10 +418,14 @@
         normalised = (
             (inputs - centre) * lax.rsqrt(spread + EPSILON) * gain_ref[...].reshape(1, chan_count)
         ).astype(jnp.bfloat16)
-        hidden = jnp.dot(normalised, win_ref[...], preferred_element_type=jnp.float32)
-        hidden = (0.5 * hidden * (1.0 + lax.erf(hidden * math.sqrt(0.5)))).astype(jnp.bfloat16)
-        result = inputs + lax.dot_general(
-            hidden, wout_ref[...], OVER_LAST, preferred_element_type=jnp.float32
+        result = inputs
+        for unit in range(rest):
+            column = rest_ref[unit : unit + 1]
+            hidden = jnp.sum(normalised.astype(jnp.float32) * column, axis=1, keepdims=True)
+            result = result + gelu(hidden).astype(jnp.float32) * rest_ref[SUB + unit : SUB + unit + 1]
+        hidden = jnp.dot(normalised, win_ref[:, :whole], preferred_element_type=jnp.float32)
+        result = result + lax.dot_general(
+            gelu(hidden), wout_ref[:, :whole], OVER_LAST, preferred_element_type=jnp.float32
         )
         out_ref[at // rows : (at + step) // rows] = result.astype(jnp.bfloat16).reshape(
             step // rows, rows, chan_count
@@ -472,6 +487,7 @@
             pltpu.VMEM((tallest, 2 * bins), f32),
             pltpu.VMEM((tallest, 2 * bins), f32),
             pltpu.VMEM((tallest, lon_count), f32),
+            pltpu.VMEM((2 * SUB, chan_count), f32),
             DMA((len(scalars) + len(operands),)),
             DMA,
             DMA((parts,)),

time: 37.3 us -> 36.5 us (0.979)
  Pallas kernels: 35.2 us -> 34.3 us
    pallas_call x1, Pallas kernels: 35.2 us -> 34.3 us  [per_device(): pl.pallas_call(functools.partial(block_body, devices, homes, sizes, freq_...]
where the time goes in v4:
time: 36.5 us; the launch traced here: 36.3 us
  Pallas kernels  34.3 us (94%)
  local copies, waits for them, and re-layouts  2.05 us (6%)
    pallas_call x1, Pallas kernels, per_device(): pl.pallas_call(functools.partial(block_body, devices, homes, sizes, freq_...  34.3 us
    unnamed x1, local copies, waits for them, and re-layouts  2.05 us

profile of v4, /device:TPU:31, one launch (start us, length us, event | category | flops | bytes accessed | tf_op | source)
XLA Modules:
  0.0 36.3 jit_solution(3586214767300985287)
XLA Ops:
  0.0 34.3 %shard_map.118 = bf16[90,4,641]{2,1,0:T(4,128)(2,1)} custom-call(s32[8]{0:T(128)} %size_hbm.1, s32[4]{0:T(128)} %band_hbm.1, bf16[90,4,641]{2,1,0:T(4,128)(2,1)} %bitcast.8, bf16[360,360]{1,0:T(8,128)(2,1)} %constant.8.clone.order_hbm, f32[8,641]{1,0:T(8,128)} %bitcast.9, f32[72,8,2,361]{3,2,1,0:T(2,128)} %bitcast.7, ...), custom_call_target="tpu_custom_call" | custom-call | tf_op jit(solution)/shard_map/pallas_call | solution.py:470
  34.3 2.0 %copy.14 = bf16[4,90,641]{2,0,1:T(4,128)(2,1)} copy(bf16[4,90,641]{2,0,1:T(4,128)(2,1)} %bitcast.5) | data formatting | bytes 923040

commit v5 on v4

--- a/solution.py
+++ b/solution.py
@@ -151,7 +151,7 @@
 
     def send_part(part):
         def send(step, carry):
-            home = lax.rem(own_home + step, homes)
+            home = step
             target = device_of(home)
             first = pl.multiple_of(home * chan + offsets[part], SUB)
 

time: 36.5 us -> 35.5 us (0.973)
  the two profiles are of different devices: /device:TPU:31 before, /device:TPU:7 now
where the time goes in v5:
time: 35.5 us; the launch traced here: 35.4 us
  Pallas kernels  33.3 us (94%)
  local copies, waits for them, and re-layouts  2.05 us (6%)
    pallas_call x1, Pallas kernels, per_device(): pl.pallas_call(functools.partial(block_body, devices, homes, sizes, freq_...  33.3 us
    unnamed x1, local copies, waits for them, and re-layouts  2.05 us

profile of v5, /device:TPU:7, one launch (start us, length us, event | category | flops | bytes accessed | tf_op | source)
XLA Modules:
  0.0 35.4 jit_solution(6767319721113264963)
XLA Ops:
  0.0 33.3 %shard_map.118 = bf16[90,4,641]{2,1,0:T(4,128)(2,1)} custom-call(s32[8]{0:T(128)} %size_hbm.1, s32[4]{0:T(128)} %band_hbm.1, bf16[90,4,641]{2,1,0:T(4,128)(2,1)} %bitcast.8, bf16[360,360]{1,0:T(8,128)(2,1)} %constant.8.clone.order_hbm, f32[8,641]{1,0:T(8,128)} %bitcast.9, f32[72,8,2,361]{3,2,1,0:T(2,128)} %bitcast.7, ...), custom_call_target="tpu_custom_call" | custom-call | tf_op jit(solution)/shard_map/pallas_call | solution.py:470
  33.3 2.0 %copy.14 = bf16[4,90,641]{2,0,1:T(4,128)(2,1)} copy(bf16[4,90,641]{2,0,1:T(4,128)(2,1)} %bitcast.5) | data formatting | bytes 923040
